TPU v7x, 32 devices: a whole 2x2x4 slice. The times are simulated.
32 devices in a mesh: seq: 4 (over z), head: 8 (over y, x, core).
Axes of the slice: x: 2, y: 2, z: 4, core: 2. Of those that a mesh axis runs over, the one named last changes fastest.
Arguments:
- inputs: bfloat16 [2048, 8192], P('seq'), may hold values from -6 to 6
- w_qkv: bfloat16 [3, 8192, 2048], P(None, None, 'head'), may hold values from -0.0625 to 0.0625
- w_out: bfloat16 [2048, 8192], P('head'), may hold values from -0.1875 to 0.1875
- turn_ids: int32 [4, 512], P('seq'), may hold values from 0 to 15, never falling along the last dimension, each value on 1 to 64 neighbouring positions
- picked: int32 [4, 64], P('seq'), may hold values from 0 to 511
- owners: int32 [256, 1], P('seq'), may hold values from 0 to 7; in each aligned block of 64 rows (0 to 63, 64 to 127, ...) at most 32 rows name the same one
- candidates: bfloat16 [2048, 8192], P(('seq', 'head')), may hold values from -0.25 to 0.25
Outputs:
- mixed: bfloat16 [2048, 8192], P('seq', 'head')
- scores: float32 [1024, 64], P(('seq', 'head'))
Inputs may be any that keep to these rules, and one draw needn't show every extreme that they name: `turn_ids`: within each session turn numbers start at 0, never fall, and each turn has 1 to 64 tokens. `owners`: among the 64 picked rows of one session no owner is named more than 32 times.
All inputs are finite; a program needn't handle non-finite values.
Results may differ from a plain program's by a relative error of at most 0.008.
Values may be sent and summed in bfloat16 or wider, within the bound.
No kernel may reach another device: no remote copies, remote signals or barrier semaphores. Data moves between devices by JAX's collectives and lax.ppermute only.
A program may use at most 128 MiB of HBM per device.

v0:
```python
import jax
import jax.numpy as jnp
from jax import lax
from jax.sharding import PartitionSpec as P

HDIM = 128


def carried_in(value, axis, join, neutral):
    count, mine = (lax.axis_size(axis), lax.axis_index(axis))
    pieces = lax.all_gather(value, axis)
    so_far = jnp.full_like(value, 0) + jnp.asarray(neutral, value.dtype)

    def lap(position, so_far):
        longer = join(so_far, pieces[position])
        return jnp.where(position < mine, longer, so_far)

    return lax.fori_loop(0, count - 1, lap, so_far)


def per_device(inputs, w_qkv, w_out, turn_ids, picked, owners, candidates):
    tokens_here = inputs.shape[0]
    model_width = inputs.shape[1]
    heads_here = w_qkv.shape[2] // HDIM
    n_head = lax.axis_size("head")
    col_count = model_width // n_head
    projected = lax.dot_general(
        inputs, w_qkv, (((1,), (1,)), ((), ())), preferred_element_type=jnp.float32
    ).astype(jnp.bfloat16)
    query = projected[:, 0].reshape(tokens_here, heads_here, HDIM)
    keys = projected[:, 1].reshape(tokens_here, heads_here, HDIM)
    values = projected[:, 2].reshape(tokens_here, heads_here, HDIM)
    states = jnp.einsum("thi,thj->hij", keys, values, preferred_element_type=jnp.float32)
    prefix = carried_in(states, "seq", jnp.add, jnp.zeros_like(states))
    prefix = prefix.astype(jnp.bfloat16)
    scores_local = jnp.einsum("thi,shi->hts", query, keys, preferred_element_type=jnp.float32)
    tok_pos = jnp.arange(tokens_here, dtype=jnp.int32)
    causal = tok_pos[:, None] >= tok_pos[None, :]
    weights = jnp.where(causal[None, :, :], scores_local, 0.0).astype(jnp.bfloat16)
    local_part = jnp.einsum("hts,shj->thj", weights, values, preferred_element_type=jnp.float32)
    carried = jnp.einsum("thi,hij->thj", query, prefix, preferred_element_type=jnp.float32)
    summed = local_part + carried
    normed = summed * lax.rsqrt(jnp.mean(summed * summed, axis=-1, keepdims=True) + 1e-05)
    attended = normed.astype(jnp.bfloat16).reshape(tokens_here, heads_here * HDIM)
    input_cols = lax.dynamic_slice_in_dim(inputs, lax.axis_index("head") * col_count, col_count, 1)
    w_cols = lax.all_to_all(w_out, "head", split_axis=1, concat_axis=0, tiled=True)
    branch = jnp.dot(
        lax.all_gather(attended, "head", axis=1, tiled=True),
        w_cols,
        preferred_element_type=jnp.float32,
    )
    mixed = (input_cols.astype(jnp.float32) + branch).astype(jnp.bfloat16)
    turn_row = turn_ids[0]
    pick_row = picked[0]
    r_dev = pick_row.shape[0]
    cap_rows = 4 * r_dev // n_head
    pick_hot = tok_pos[None, :] == pick_row[:, None]
    sel_turn = jnp.sum(jnp.where(pick_hot, turn_row[None, :], 0), axis=1)
    member = (turn_row[None, :] == sel_turn[:, None]) & (tok_pos[None, :] <= pick_row[:, None])
    row_count = jnp.sum(member.astype(jnp.float32), axis=1)
    pooled = jnp.dot(member.astype(jnp.bfloat16), mixed, preferred_element_type=jnp.float32)
    summary = (pooled / row_count[:, None]).astype(jnp.bfloat16)
    owner_row = owners[:, 0]
    row_pos = jnp.arange(r_dev, dtype=jnp.int32)
    head_pos = jnp.arange(n_head, dtype=jnp.int32)
    own_hot = (owner_row[:, None] == head_pos[None, :]).astype(jnp.int32)
    before = (row_pos[:, None] > row_pos[None, :]).astype(jnp.int32)
    slot_rank = jnp.sum(jnp.dot(before, own_hot) * own_hot, axis=1)
    slot_index = owner_row * cap_rows + slot_rank
    dispatch = (
        slot_index[None, :] == jnp.arange(n_head * cap_rows, dtype=jnp.int32)[:, None]
    ).astype(jnp.bfloat16)
    outgoing = jnp.dot(dispatch, summary, preferred_element_type=jnp.float32).astype(jnp.bfloat16)
    outgoing = outgoing.reshape(n_head, cap_rows, col_count)
    cand_parts = candidates.reshape(candidates.shape[0], n_head, col_count)
    scores = jnp.einsum(
        "skc,nsc->kn",
        lax.all_to_all(outgoing, "head", split_axis=0, concat_axis=0, tiled=True),
        cand_parts,
        preferred_element_type=jnp.float32,
    )
    return (mixed, scores)


def solution(mesh):
    return jax.shard_map(
        per_device,
        mesh=mesh,
        in_specs=(
            P("seq", None),
            P(None, None, "head"),
            P("head", None),
            P("seq", None),
            P("seq", None),
            P("seq", None),
            P(("seq", "head"), None),
        ),
        out_specs=(P("seq", "head"), P(("seq", "head"), None)),
        check_vma=False,
    )
```

profile of v0, /device:TPU:0, one launch (start us, length us, event | category | flops | bytes accessed | tf_op | source)
XLA Modules:
  0.0 109.3 jit_solution(5474585538032914516)
XLA Ops:
  7.2 6.4 %copy.43 = bf16[256,8192]{0,1:T(8,128)(2,1)} copy(bf16[256,8192]{1,0:T(8,128)(2,1)} %param.11) | data formatting | bytes 8388608 | tf_op args[2]
  13.6 5.2 %all-to-all-start = ((bf16[256,8,1024]{0,2,1:T(8,128)(2,1)}), bf16[256,8,1024]{0,2,1:T(8,128)(2,1)}, u32[]{:S(2)}, u32[]{:S(2)}) async-start(bf16[256,8,1024]{0,2,1:T(8,128)(2,1)} %bitcast.41), calls=%async_computation | async-start | bytes 8388608 | tf_op jit(solution)/shard_map/all_to_all | solution.py:46
  18.8 0.0 all-gather.3.cloned.1.call-start
  18.8 0.1 iota_compare_fusion
  18.9 12.2 %fusion.2 = bf16[512,3,256]{0,2,1:T(8,128)(2,1)S(1)} fusion(bf16[3,8192,256]{2,1,0:T(8,128)(2,1)} %param.10, bf16[512,8192]{1,0:T(8,128)(2,1)} %param.9), kind=kOutput, calls=%fused_computation.5 | convolution fusion | flops 6442844160 | bytes 21757952 | tf_op jit(solution)/shard_map/dot_general | solution.py:27
  31.1 0.1 fusion.29
  31.1 0.0 copy-start.3
  31.1 0.0 copy-start
  31.2 0.0 copy-start.1
  31.2 0.2 fusion.30
  31.4 17.1 %all-gather = f32[8,128,128]{2,1,0:T(8,128)S(1)} all-gather(f32[2,128,128]{2,1,0:T(8,128)S(1)} %fusion.30), channel_id=2, replica_groups=mesh['seq'=4,'head'=8] {'seq'}, dimensions={0}, use_global_device_ids=true | all-gather | bytes 655360 | tf_op jit(solution)/shard_map/all_gather | solution.py:11
  48.5 0.2 while.14
  48.7 0.3 fusion.23
  49.0 0.8 multiply_reduce_fusion
  49.8 0.7 multiply_convert_fusion
  50.5 0.0 all-gather.3.cloned.1.call-update
  50.6 0.0 copy-done.3
  50.6 0.1 fusion.9
  50.7 0.0 copy-done
  50.7 0.0 copy-done.1
  50.7 0.2 select_reduce_fusion
  50.9 0.2 convert_reduce_fusion
  51.1 19.6 %all-to-all-done = bf16[256,8,1024]{0,2,1:T(8,128)(2,1)} async-done(((bf16[256,8,1024]{0,2,1:T(8,128)(2,1)}), bf16[256,8,1024]{0,2,1:T(8,128)(2,1)}, u32[]{:S(2)}, u32[]{:S(2)}) %all-to-all-start) | async-done | bytes 4194336 | tf_op jit(solution)/shard_map/all_to_all | solution.py:46
  70.8 6.5 %copy.44 = bf16[8,256,1024]{2,1,0:T(8,128)(2,1)} copy(bf16[8,256,1024]{1,2,0:T(8,128)(2,1)} %bitcast.8) | data formatting | bytes 8388608 | tf_op jit(solution)/shard_map/all_to_all | solution.py:46
  77.2 5.9 %all-gather.3.cloned.1.call-done = bf16[512,2048]{0,1:T(8,128)(2,1)} async-done(((bf16[512,256]{0,1:T(8,128)(2,1)}), bf16[512,2048]{0,1:T(8,128)(2,1)}) %all-gather.3.cloned.1.call-update) | async-done | bytes 2097168 | tf_op jit(solution)/shard_map/all_gather | solution.py:48
  83.1 5.5 %add_convert_fusion = bf16[512,1024]{1,0:T(8,128)(2,1)S(1)} fusion(bf16[512,2048]{0,1:T(8,128)(2,1)} %all-gather.3.cloned.1.call-done, bf16[2048,1024]{1,0:T(8,128)(2,1)} %bitcast.42, bf16[512,8192]{1,0:T(8,128)(2,1)} %param.9, s32[]{:T(128)S(6)} %select_n.32), kind=kOutput, calls=%fused_computation.3 | convolution fusion | flops 2149056512 | bytes 8388612 | tf_op jit(solution)/shard_map/dot_general | solution.py:47
  88.6 0.0 copy-start.4
  88.6 0.5 convolution_convert_fusion
  89.2 12.3 %all_to_all.24 = bf16[8,32,1024]{2,1,0:T(8,128)(2,1)S(1)} all-to-all(bf16[8,32,1024]{2,1,0:T(8,128)(2,1)S(1)} %bitcast.51), channel_id=1, replica_groups=mesh['seq'=4,'head'=8] {'head'}, dimensions={0} | all-to-all | bytes 1048576 | tf_op jit(solution)/shard_map/all_to_all | solution.py:78
  101.4 0.0 copy-done.2
  101.4 1.0 convolution_bitcast_fusion
  102.5 0.0 copy-done.4
  (7 shorter events, 0.1 us)
Async XLA Ops:
  13.6 57.2 %all-to-all-start = ((bf16[256,8,1024]{0,2,1:T(8,128)(2,1)}), bf16[256,8,1024]{0,2,1:T(8,128)(2,1)}, u32[]{:S(2)}, u32[]{:S(2)}) async-start(bf16[256,8,1024]{0,2,1:T(8,128)(2,1)} %bitcast.41), calls=%async_computation | async-start | bytes 8388608 | tf_op jit(solution)/shard_map/all_to_all | solution.py:46
  18.8 64.3 %all-gather.3.cloned.1.call-start = ((), (), s32[]{:S(2)}) async-start(), calls=%async_computation.2 | async-start | bytes 2359296 | tf_op jit(solution)/shard_map/all_gather | solution.py:48
  31.1 19.4 %copy-start.3 = (s32[64,1]{0,1:T(1,128)S(1)}, s32[64,1]{0,1:T(1,128)}, u32[]{:S(2)}) copy-start(s32[64,1]{0,1:T(1,128)} %param.14) | copy-start | bytes 772
  31.1 19.6 %copy-start = (s32[1,512]{1,0:T(1,128)S(1)}, s32[1,512]{1,0:T(1,128)}, u32[]{:S(2)}) copy-start(s32[1,512]{1,0:T(1,128)} %param.12) | copy-start | bytes 6148
  31.2 19.6 %copy-start.1 = (s32[1,64]{1,0:T(1,128)S(1)}, s32[1,64]{1,0:T(1,128)}, u32[]{:S(2)}) copy-start(s32[1,64]{1,0:T(1,128)} %param.13) | copy-start | bytes 772
  83.1 18.3 %copy-start.2 = (bf16[64,8192]{1,0:T(8,128)(2,1)S(1)}, bf16[64,8192]{1,0:T(8,128)(2,1)}, u32[]{:S(2)}) copy-start(bf16[64,8192]{1,0:T(8,128)(2,1)} %param.15) | copy-start | bytes 3145732
  88.6 13.8 %copy-start.4 = (bf16[512,1024]{1,0:T(8,128)(2,1)}, bf16[512,1024]{1,0:T(8,128)(2,1)S(1)}, u32[]{:S(2)}) copy-start(bf16[512,1024]{1,0:T(8,128)(2,1)S(1)} %add_convert_fusion) | copy-start | bytes 3145732
Sparse Core Ops, SparseCore 0:
  50.7 32.3 all-gather.2
where the time goes:
time: 110 us; the launch traced here: 109 us
  blocking collectives  29.4 us (27%)
  waiting for transfers between devices  25.5 us (23%)
  matrix products  20.7 us (19%)
  between operations  14.2 us (13%)
  local copies, waits for them, and re-layouts  13 us (12%)
  starting transfers between devices  5.23 us (5%)
  other arithmetic  1.34 us (1%)
    all_to_all x1, waiting for transfers between devices, per_device(): lax.all_to_all(w_out, 'head', split_axis=1, concat_axis=0, tiled=True)  19.6 us
    all_gather x1, blocking collectives, carried_in(): pieces = lax.all_gather(value, axis)  17.1 us
    all_to_all x1, blocking collectives, per_device(): lax.all_to_all(outgoing, 'head', split_axis=0, concat_axis=0, tiled=True)  12.3 us
    dot_general x1, matrix products, per_device(): lax.dot_general(inputs, w_qkv, (((1,), (1,)), ((), ())), preferred_elemen...  12.2 us
    all_to_all x1, local copies, waits for them, and re-layouts, per_device(): lax.all_to_all(w_out, 'head', split_axis=1, concat_axis=0, tiled=True)  6.48 us
    unnamed x11, local copies, waits for them, and re-layouts  6.43 us
    all_gather x1, waiting for transfers between devices, per_device(): lax.all_gather(attended, 'head', axis=1, tiled=True)  5.86 us
    dot_general x1, matrix products, per_device(): jnp.dot(lax.all_gather(attended, 'head', axis=1, tiled=True), w_cols, pre...  5.52 us
  transfers between devices with their start and end apart: 2, of which 2 were waited for; matrix products, arithmetic and copies ran while one was open for 20% of the time, Pallas kernels for 0%

commit v1 on v0

--- a/solution.py
+++ b/solution.py
@@ -43,7 +43,9 @@
     normed = summed * lax.rsqrt(jnp.mean(summed * summed, axis=-1, keepdims=True) + 1e-05)
     attended = normed.astype(jnp.bfloat16).reshape(tokens_here, heads_here * HDIM)
     input_cols = lax.dynamic_slice_in_dim(inputs, lax.axis_index("head") * col_count, col_count, 1)
-    w_cols = lax.all_to_all(w_out, "head", split_axis=1, concat_axis=0, tiled=True)
+    w_cols = jnp.concatenate(
+        lax.all_to_all(jnp.stack(jnp.split(w_out, lax.axis_size("head"), 1), 0), "head", 0, 0), 0
+    )
     branch = jnp.dot(
         lax.all_gather(attended, "head", axis=1, tiled=True),
         w_cols,

time: 110 us -> 140 us (1.27)
  waiting for transfers between devices: 25.5 us -> 53.8 us
  local copies, waits for them, and re-layouts: 13 us -> 15.2 us
    all_to_all x1, waiting for transfers between devices: 19.6 us -> 39 us  [per_device(): lax.all_to_all(jnp.stack(jnp.split(w_out, lax.axis_size('head'), 1), 0),...]
    all_gather x1, waiting for transfers between devices: 5.86 us -> 14.8 us  [per_device(): lax.all_gather(attended, 'head', axis=1, tiled=True)]
    unnamed x11 -> x17, local copies, waits for them, and re-layouts: 6.43 us -> 13.2 us
    all_to_all x1 -> x0, local copies, waits for them, and re-layouts: 6.48 us -> none  [per_device(): lax.all_to_all(w_out, 'head', split_axis=1, concat_axis=0, tiled=True)]
    another operation x0 -> x1, local copies, waits for them, and re-layouts: none -> 1.89 us  [per_device(): jnp.stack(jnp.split(w_out, lax.axis_size('head'), 1), 0)]
  transfers between devices with their start and end apart: 2 -> 2, of which waited for: 2 -> 2; matrix products, arithmetic and copies ran while one was open for 20% -> 11% of each run, Pallas kernels for 0% -> 0%
where the time goes in v1:
time: 140 us; the launch traced here: 139 us
  waiting for transfers between devices  53.8 us (38%)
  blocking collectives  29.5 us (21%)
  matrix products  20.6 us (15%)
  local copies, waits for them, and re-layouts  15.2 us (11%)
  between operations  14.2 us (10%)
  starting transfers between devices  4.7 us (3%)
    all_to_all x1, waiting for transfers between devices, per_device(): lax.all_to_all(jnp.stack(jnp.split(w_out, lax.axis_size('head'), 1), 0),...  39 us
    all_gather x1, blocking collectives, carried_in(): pieces = lax.all_gather(value, axis)  17.4 us
    all_gather x1, waiting for transfers between devices, per_device(): lax.all_gather(attended, 'head', axis=1, tiled=True)  14.8 us
    unnamed x17, local copies, waits for them, and re-layouts  13.2 us
    dot_general x1, matrix products, per_device(): lax.dot_general(inputs, w_qkv, (((1,), (1,)), ((), ())), preferred_elemen...  12.2 us
    all_to_all x1, blocking collectives, per_device(): lax.all_to_all(outgoing, 'head', split_axis=0, concat_axis=0, tiled=True)  12.1 us
    dot_general x1, matrix products, per_device(): jnp.dot(lax.all_gather(attended, 'head', axis=1, tiled=True), w_cols, pre...  5.52 us
    all_to_all x1, starting transfers between devices, per_device(): lax.all_to_all(jnp.stack(jnp.split(w_out, lax.axis_size('head'), 1), 0),...  4.67 us
  transfers between devices with their start and end apart: 2, of which 2 were waited for; matrix products, arithmetic and copies ran while one was open for 11% of the time, Pallas kernels for 0%

profile of v1, /device:TPU:0, one launch (start us, length us, event | category | flops | bytes accessed | tf_op | source)
XLA Modules:
  0.0 139.4 jit_solution(8883536109682802164)
XLA Ops:
  7.2 0.0 all-gather.3.cloned.1.call-start
  7.2 0.1 iota_compare_fusion
  7.3 12.2 %fusion.2 = bf16[512,3,256]{0,2,1:T(8,128)(2,1)S(1)} fusion(bf16[3,8192,256]{2,1,0:T(8,128)(2,1)} %param.10, bf16[512,8192]{1,0:T(8,128)(2,1)} %param.9), kind=kOutput, calls=%fused_computation.5 | convolution fusion | flops 6442844160 | bytes 21757952 | tf_op jit(solution)/shard_map/dot_general | solution.py:27
  19.5 0.1 fusion.29
  19.5 0.2 fusion.30
  19.8 17.4 %all-gather = f32[8,128,128]{2,1,0:T(8,128)S(1)} all-gather(f32[2,128,128]{2,1,0:T(8,128)S(1)} %fusion.30), channel_id=2, replica_groups=mesh['seq'=4,'head'=8] {'seq'}, dimensions={0}, use_global_device_ids=true | all-gather | bytes 655360 | tf_op jit(solution)/shard_map/all_gather | solution.py:11
  37.1 0.2 while.14
  37.3 0.3 fusion.23
  37.6 0.8 multiply_reduce_fusion
  38.4 0.7 multiply_convert_fusion
  39.2 0.0 all-gather.3.cloned.1.call-update
  39.2 1.9 %bitcast_dynamic-update-slice_fusion.7 = bf16[8,256,1024]{2,1,0:T(8,128)(2,1)} fusion(bf16[256,8192]{1,0:T(8,128)(2,1)} %param.11), kind=kLoop, calls=%fused_computation.27 | loop fusion | bytes 1048576
  41.1 1.9 %bitcast_dynamic-update-slice_fusion.6 = bf16[8,256,1024]{2,1,0:T(8,128)(2,1)} fusion(bf16[8,256,1024]{2,1,0:T(8,128)(2,1)} %bitcast_dynamic-update-slice_fusion.7, bf16[256,8192]{1,0:T(8,128)(2,1)} %param.11), kind=kLoop, calls=%fused_computation.26 | loop fusion | bytes 1048576
  42.9 1.9 %bitcast_dynamic-update-slice_fusion.5 = bf16[8,256,1024]{2,1,0:T(8,128)(2,1)} fusion(bf16[8,256,1024]{2,1,0:T(8,128)(2,1)} %bitcast_dynamic-update-slice_fusion.6, bf16[256,8192]{1,0:T(8,128)(2,1)} %param.11), kind=kLoop, calls=%fused_computation.25 | loop fusion | bytes 1048576
  44.8 1.9 %bitcast_dynamic-update-slice_fusion.4 = bf16[8,256,1024]{2,1,0:T(8,128)(2,1)} fusion(bf16[8,256,1024]{2,1,0:T(8,128)(2,1)} %bitcast_dynamic-update-slice_fusion.5, bf16[256,8192]{1,0:T(8,128)(2,1)} %param.11), kind=kLoop, calls=%fused_computation.24 | loop fusion | bytes 1048576
  46.7 1.9 %bitcast_dynamic-update-slice_fusion.3 = bf16[8,256,1024]{2,1,0:T(8,128)(2,1)} fusion(bf16[8,256,1024]{2,1,0:T(8,128)(2,1)} %bitcast_dynamic-update-slice_fusion.4, bf16[256,8192]{1,0:T(8,128)(2,1)} %param.11), kind=kLoop, calls=%fused_computation.23 | loop fusion | bytes 1048576
  48.6 1.9 %bitcast_dynamic-update-slice_fusion.2 = bf16[8,256,1024]{2,1,0:T(8,128)(2,1)} fusion(bf16[8,256,1024]{2,1,0:T(8,128)(2,1)} %bitcast_dynamic-update-slice_fusion.3, bf16[256,8192]{1,0:T(8,128)(2,1)} %param.11), kind=kLoop, calls=%fused_computation.22 | loop fusion | bytes 1048576
  50.5 1.9 %bitcast_dynamic-update-slice_fusion.1 = bf16[8,256,1024]{2,1,0:T(8,128)(2,1)} fusion(bf16[8,256,1024]{2,1,0:T(8,128)(2,1)} %bitcast_dynamic-update-slice_fusion.2, bf16[256,8192]{1,0:T(8,128)(2,1)} %param.11), kind=kLoop, calls=%fused_computation.21 | loop fusion | bytes 1048576
  52.4 1.9 %bitcast_dynamic-update-slice_fusion = bf16[8,256,1024]{2,1,0:T(8,128)(2,1)} fusion(bf16[8,256,1024]{2,1,0:T(8,128)(2,1)} %bitcast_dynamic-update-slice_fusion.1, bf16[256,8192]{1,0:T(8,128)(2,1)} %param.11), kind=kLoop, calls=%fused_computation.20 | loop fusion | bytes 1048576 | tf_op jit(solution)/shard_map/stack | solution.py:47
  54.3 4.7 %all-to-all-start = ((bf16[8,256,1024]{2,1,0:T(8,128)(2,1)}), bf16[8,256,1024]{2,1,0:T(8,128)(2,1)}, u32[]{:S(2)}, u32[]{:S(2)}) async-start(bf16[8,256,1024]{2,1,0:T(8,128)(2,1)} %bitcast_dynamic-update-slice_fusion), calls=%async_computation | async-start | bytes 8388608 | tf_op jit(solution)/shard_map/all_to_all | solution.py:47
  59.0 0.0 copy-done.3
  59.0 0.1 fusion.9
  59.1 0.0 copy-done
  59.1 0.2 select_reduce_fusion
  59.3 0.2 convert_reduce_fusion
  59.5 14.8 %all-gather.3.cloned.1.call-done = bf16[512,2048]{0,1:T(8,128)(2,1)} async-done(((bf16[512,256]{0,1:T(8,128)(2,1)}), bf16[512,2048]{0,1:T(8,128)(2,1)}) %all-gather.3.cloned.1.call-update) | async-done | bytes 2097168 | tf_op jit(solution)/shard_map/all_gather | solution.py:50
  74.4 39.0 %all-to-all-done = bf16[8,256,1024]{2,1,0:T(8,128)(2,1)} async-done(((bf16[8,256,1024]{2,1,0:T(8,128)(2,1)}), bf16[8,256,1024]{2,1,0:T(8,128)(2,1)}, u32[]{:S(2)}, u32[]{:S(2)}) %all-to-all-start) | async-done | bytes 4194336 | tf_op jit(solution)/shard_map/all_to_all | solution.py:47
  113.3 5.5 %add_convert_fusion = bf16[512,1024]{1,0:T(8,128)(2,1)S(1)} fusion(bf16[512,2048]{0,1:T(8,128)(2,1)} %all-gather.3.cloned.1.call-done, bf16[2048,1024]{1,0:T(8,128)(2,1)} %bitcast.15, bf16[512,8192]{1,0:T(8,128)(2,1)} %param.9, s32[]{:T(128)S(6)} %select_n.32), kind=kOutput, calls=%fused_computation.3 | convolution fusion | flops 2149056512 | bytes 8388612 | tf_op jit(solution)/shard_map/dot_general | solution.py:49
  118.9 0.0 copy-start.4
  118.9 0.5 convolution_convert_fusion
  119.4 12.1 %all_to_all.10 = bf16[8,32,1024]{2,1,0:T(8,128)(2,1)S(1)} all-to-all(bf16[8,32,1024]{2,1,0:T(8,128)(2,1)S(1)} %bitcast.63), channel_id=1, replica_groups=mesh['seq'=4,'head'=8] {'head'}, dimensions={0} | all-to-all | bytes 1048576 | tf_op jit(solution)/shard_map/all_to_all | solution.py:80
  131.5 1.0 convolution_bitcast_fusion
  (13 shorter events, 0.2 us)
Async XLA Ops:
  7.2 67.2 %all-gather.3.cloned.1.call-start = ((), (), s32[]{:S(2)}) async-start(), calls=%async_computation.2 | async-start | bytes 2359296 | tf_op jit(solution)/shard_map/all_gather | solution.py:50
  54.3 4.7 %copy-start.3 = (s32[64,1]{0,1:T(1,128)S(1)}, s32[64,1]{0,1:T(1,128)}, u32[]{:S(2)}) copy-start(s32[64,1]{0,1:T(1,128)} %param.14) | copy-start | bytes 772
  54.3 4.8 %copy-start = (s32[1,512]{1,0:T(1,128)S(1)}, s32[1,512]{1,0:T(1,128)}, u32[]{:S(2)}) copy-start(s32[1,512]{1,0:T(1,128)} %param.12) | copy-start | bytes 6148
  54.3 4.8 %copy-start.1 = (s32[1,64]{1,0:T(1,128)S(1)}, s32[1,64]{1,0:T(1,128)}, u32[]{:S(2)}) copy-start(s32[1,64]{1,0:T(1,128)} %param.13) | copy-start | bytes 772
  54.3 59.0 %all-to-all-start = ((bf16[8,256,1024]{2,1,0:T(8,128)(2,1)}), bf16[8,256,1024]{2,1,0:T(8,128)(2,1)}, u32[]{:S(2)}, u32[]{:S(2)}) async-start(bf16[8,256,1024]{2,1,0:T(8,128)(2,1)} %bitcast_dynamic-update-slice_fusion), calls=%async_computation | async-start | bytes 8388608 | tf_op jit(solution)/shard_map/all_to_all | solution.py:47
  113.3 18.2 %copy-start.2 = (bf16[64,8192]{1,0:T(8,128)(2,1)S(1)}, bf16[64,8192]{1,0:T(8,128)(2,1)}, u32[]{:S(2)}) copy-start(bf16[64,8192]{1,0:T(8,128)(2,1)} %param.15) | copy-start | bytes 3145732
  118.9 13.7 %copy-start.4 = (bf16[512,1024]{1,0:T(8,128)(2,1)}, bf16[512,1024]{1,0:T(8,128)(2,1)S(1)}, u32[]{:S(2)}) copy-start(bf16[512,1024]{1,0:T(8,128)(2,1)S(1)} %add_convert_fusion) | copy-start | bytes 3145732
Sparse Core Ops, SparseCore 0:
  39.3 35.0 all-gather.2
